TPU v7x, 32 devices: a whole 2x2x4 slice. The times are simulated.
32 devices in a mesh: visit: 2 (over x), patch: 16 (over z, y, core).
Axes of the slice: x: 2, y: 2, z: 4, core: 2. Of those that a mesh axis runs over, the one named last changes fastest.
Arguments:
- images: bfloat16 [2, 96, 128, 512], P('visit', 'patch'), may hold values from -12 to 12
- coefficients: float32 [2, 96, 3, 40], P('visit', 'patch'), may hold values from -2 to 2
- intersection: int32 [2, 96, 2], P('visit'), may hold values from 0 to 15, as said below
- row_offset: int32 [2, 96], P('visit'), may hold values from 0 to 7
- col_offset: int32 [2, 96], P('visit'), may hold values from 0 to 511
- shifts: float32 [2, 96, 2], P('visit'), may hold values from 0 to 1
- inv_var: float32 [2, 96], P('visit'), may hold values from 0.3 to 3
Outputs:
- coadd: float32 [128, 8192], P('visit', 'patch')
- detection: float32 [128, 8192], P('visit', 'patch')
Inputs may be any that keep to these rules, and one draw needn't show every extreme that they name: intersection[v, c, 1] = intersection[v, c, 0] + 1. Within each aligned block of 6 exposures of a visit (c from b * 6 to (b + 1) * 6 - 1), no patch is named twice.
All inputs are finite; a program needn't handle non-finite values.
Results may differ from a plain program's by a relative error of at most 0.0061.
Values may be sent and summed in bfloat16 or wider, within the bound.
No kernel may reach another device: no remote copies, remote signals or barrier semaphores. Data moves between devices by JAX's collectives and lax.ppermute only.
A program may use at most 128 MiB of HBM per device.

v0:
```python
import jax
import jax.numpy as jnp
from jax import lax
from jax.sharding import PartitionSpec as P

KRAD = 10
DRAD = 4
WIDTHS_PX = (1.0, 1.7, 2.6, 3.6)


def extended(array, sides, width):
    for axis, dim in sides:
        peers, length = (lax.axis_size(axis), array.shape[dim])
        up = [(i, (i + 1) % peers) for i in range(peers - 1)]
        down = [(j, i) for i, j in up]
        last = lax.slice_in_dim(array, length - width, length, axis=dim)
        initial = lax.slice_in_dim(array, 0, width, axis=dim)
        before = lax.ppermute(last, axis, up)
        after = lax.ppermute(initial, axis, down)
        array = jnp.concatenate([before, array, after], axis=dim)
    return array


def kernel_value(offsets, width_px, degree):
    scaled = offsets / width_px
    return scaled**degree * jnp.exp(-offsets * offsets / (2.0 * width_px * width_px))


def band_tables(radius, extent):
    offsets = jnp.arange(-radius, radius + 1).astype(jnp.float32)
    distance = (jnp.arange(extent)[None, :] - jnp.arange(extent)[:, None]).astype(jnp.float32)
    inside = jnp.abs(distance) <= radius
    tables = []
    for group in range(4):
        for degree in range(4):
            profile = kernel_value(offsets, WIDTHS_PX[group], degree)
            norm_value = jnp.sqrt(jnp.sum(profile * profile))
            values = kernel_value(distance, WIDTHS_PX[group], degree) / norm_value
            tables.append(jnp.where(inside, values, 0.0).astype(jnp.bfloat16))
    return jnp.stack(tables).reshape(4, 4, extent, extent)


def match_exposure(exposure, weights, row_band, col_band, row_pos, col_pos):
    smoothed = jnp.einsum(
        "gdri,iw->gdrw", row_band, exposure, preferred_element_type=jnp.float32
    ).astype(jnp.bfloat16)
    matched = jnp.zeros(exposure.shape, jnp.float32)
    term = 0
    for group in range(4):
        for x_degree in range(4):
            count = 4 - x_degree
            response = jnp.einsum(
                "drw,xw->drx",
                smoothed[group, :count],
                col_band[group, x_degree],
                preferred_element_type=jnp.float32,
            )
            picked = weights[:, term : term + count]
            steady = jnp.sum(picked[0][:, None, None] * response, 0)
            along_rows = jnp.sum(picked[1][:, None, None] * response, 0)
            along_cols = jnp.sum(picked[2][:, None, None] * response, 0)
            matched = (
                matched + steady + row_pos[:, None] * along_rows + col_pos[None, :] * along_cols
            )
            term += count
    return matched.astype(jnp.bfloat16)


def warp_exposure(exposure, row_shift, col_shift, frac_row, frac_col, weight):
    row_count, col_count = exposure.shape
    nothing = jnp.zeros((), jnp.bfloat16)
    upper = (1.0 - frac_row).astype(jnp.bfloat16)
    lower = frac_row.astype(jnp.bfloat16)
    left = (1.0 - frac_col).astype(jnp.bfloat16)
    right = frac_col.astype(jnp.bfloat16)
    target_row = jnp.arange(row_count)[:, None]
    source_row = jnp.arange(row_count)[None, :]
    row_map = jnp.where(source_row == target_row - row_shift, upper, nothing) + jnp.where(
        source_row == target_row - row_shift - 1, lower, nothing
    )
    source_col = jnp.arange(col_count)[:, None]
    target_col = jnp.arange(col_count)[None, :]
    col_map = jnp.where(source_col == target_col - col_shift, left, nothing) + jnp.where(
        source_col == target_col - col_shift - 1, right, nothing
    )
    middle = jnp.dot(row_map, exposure, preferred_element_type=jnp.float32).astype(jnp.bfloat16)
    warped = jnp.dot(middle, col_map, preferred_element_type=jnp.float32)
    row_cover = jnp.sum(row_map.astype(jnp.float32), 1)
    col_cover = jnp.sum(col_map.astype(jnp.float32), 0)
    return (weight * warped, weight * row_cover[:, None] * col_cover[None, :])


def detect(framed, radius):
    offsets = jnp.arange(-radius, radius + 1).astype(jnp.float32)
    profile = jnp.exp(-offsets * offsets / 8.0)
    profile = profile / jnp.sqrt(jnp.sum(profile * profile))
    row_count = framed.shape[0] - 2 * radius
    col_count = framed.shape[1] - 2 * radius
    across = jnp.zeros((row_count, framed.shape[1]), jnp.float32)
    for tap_idx in range(2 * radius + 1):
        across = across + profile[tap_idx] * framed[tap_idx : tap_idx + row_count]
    result = jnp.zeros((row_count, col_count), jnp.float32)
    for tap_idx in range(2 * radius + 1):
        result = result + profile[tap_idx] * across[:, tap_idx : tap_idx + col_count]
    return result


def local(images, coefficients, intersection, row_offset, col_offset, shifts, inv_var):
    exposures = images[0]
    weights_all = coefficients[0]
    row_count = exposures.shape[1]
    col_count = exposures.shape[2]
    table = intersection[0]
    row_shifts = row_offset[0]
    col_shifts = col_offset[0]
    fractions = shifts[0]
    inverse = inv_var[0]
    own_patch = lax.axis_index("patch")
    row_band = band_tables(KRAD, row_count)
    col_band = band_tables(KRAD, col_count)
    row_pos = (2.0 * jnp.arange(row_count).astype(jnp.float32) + 1.0) / row_count - 1.0
    col_pos = (2.0 * jnp.arange(col_count).astype(jnp.float32) + 1.0) / col_count - 1.0
    matched = lax.map(
        lambda operands: match_exposure(
            operands[0], operands[1], row_band, col_band, row_pos, col_pos
        ),
        (exposures, weights_all),
    )
    empty = (
        jnp.zeros((row_count, col_count), jnp.float32),
        jnp.zeros((row_count, col_count), jnp.float32),
    )

    def add_exposure(totals, exposure, ccd, hit_first):
        col_shift = jnp.where(hit_first, col_shifts[ccd], col_shifts[ccd] - col_count)
        flux_part, cover_part = warp_exposure(
            exposure, row_shifts[ccd], col_shift, fractions[ccd, 0], fractions[ccd, 1], inverse[ccd]
        )
        return (totals[0] + flux_part, totals[1] + cover_part)

    arrived = lax.all_gather(matched, "patch", axis=0, tiled=True)

    def visit_one(offset, inner):
        hit_first = table[offset, 0] == own_patch
        hit_second = table[offset, 1] == own_patch
        exposure = lax.dynamic_index_in_dim(arrived, offset, 0, keepdims=False)
        return lax.cond(
            hit_first | hit_second,
            lambda: add_exposure(inner, exposure, offset, hit_first),
            lambda: inner,
        )

    flux_sum, cover_sum = lax.fori_loop(0, arrived.shape[0], visit_one, empty)
    flux_part, cover_part = (
        lax.psum_scatter(flux_sum, "visit", scatter_dimension=0, tiled=True),
        lax.psum_scatter(cover_sum, "visit", scatter_dimension=0, tiled=True),
    )
    coadd = flux_part / jnp.maximum(cover_part, 1.0)
    framed = extended(coadd, (("visit", 0), ("patch", 1)), DRAD)
    detection = detect(framed, DRAD)
    return (coadd, detection)


def solution(mesh):
    return jax.shard_map(
        local,
        mesh=mesh,
        in_specs=(
            P("visit", "patch", None, None),
            P("visit", "patch", None, None),
            P("visit", None, None),
            P("visit", None),
            P("visit", None),
            P("visit", None, None),
            P("visit", None),
        ),
        out_specs=(P("visit", "patch"), P("visit", "patch")),
        check_vma=False,
    )
```

profile of v0, /device:TPU:5, one launch (start us, length us, event | category | flops | bytes accessed | tf_op | source)
XLA Modules:
  0.0 671.8 jit_solution(11030103022260496552)
XLA Ops:
  51.3 119.2 %while.28 = (s32[]{:T(128)}, bf16[6,128,512]{2,1,0:T(8,128)(2,1)S(1)}, f32[6,3,40]{2,1,0:T(4,128)S(1)}, bf16[6,128,512]{1,2,0:T(8,128)(2,1)S(1)}, bf16[4,4,128,1...) while((s32[]{:T(128)}, ...), condition=%wide.region_53.54_spmd.clone.clone, body=%wide.region_16.53_spmd.clone.clone.sunk | while | flops 2971667456 | bytes 70542368 | solution.py:123
  52.3 2.0 multiply_reduce_fusion.58
  62.8 8.5 %fusion.219 = bf16[6,128,512]{2,1,0:T(8,128)(2,1)S(1)} fusion(bf16[6,128,512]{2,1,0:T(8,128)(2,1)S(1)} %get-tuple-element.857, s32[]{:T(128)} %get-tuple-element.856, bf16[4,4,512,512]{3,2,1,0:T(8,128)(2,1)S(1)} %copy-done, f32[128,512]{1,0:T(8,128)S(1)} %get-tuple-element.764, f32[128,512]{1,0:T(8,128)S(1)} %get-tuple-element.765, ...), kind=kOutput, calls=%fused_computation.133.clone.1 | convolution fusion | flops 73138176 | bytes 11012660 | tf_op jit(solution)/shard_map/while/body/eval_jaxpr/drw,xw->drx/dot_general | solution.py:52
  72.2 2.0 multiply_reduce_fusion.58
  82.6 8.5 %fusion.219 = bf16[6,128,512]{2,1,0:T(8,128)(2,1)S(1)} fusion(bf16[6,128,512]{2,1,0:T(8,128)(2,1)S(1)} %get-tuple-element.857, s32[]{:T(128)} %get-tuple-element.856, bf16[4,4,512,512]{3,2,1,0:T(8,128)(2,1)S(1)} %copy-done, f32[128,512]{1,0:T(8,128)S(1)} %get-tuple-element.764, f32[128,512]{1,0:T(8,128)S(1)} %get-tuple-element.765, ...), kind=kOutput, calls=%fused_computation.133.clone.1 | convolution fusion | flops 73138176 | bytes 11012660 | tf_op jit(solution)/shard_map/while/body/eval_jaxpr/drw,xw->drx/dot_general | solution.py:52
  92.0 2.0 multiply_reduce_fusion.58
  102.4 8.5 %fusion.219 = bf16[6,128,512]{2,1,0:T(8,128)(2,1)S(1)} fusion(bf16[6,128,512]{2,1,0:T(8,128)(2,1)S(1)} %get-tuple-element.857, s32[]{:T(128)} %get-tuple-element.856, bf16[4,4,512,512]{3,2,1,0:T(8,128)(2,1)S(1)} %copy-done, f32[128,512]{1,0:T(8,128)S(1)} %get-tuple-element.764, f32[128,512]{1,0:T(8,128)S(1)} %get-tuple-element.765, ...), kind=kOutput, calls=%fused_computation.133.clone.1 | convolution fusion | flops 73138176 | bytes 11012660 | tf_op jit(solution)/shard_map/while/body/eval_jaxpr/drw,xw->drx/dot_general | solution.py:52
  111.8 2.0 multiply_reduce_fusion.58
  122.3 8.5 %fusion.219 = bf16[6,128,512]{2,1,0:T(8,128)(2,1)S(1)} fusion(bf16[6,128,512]{2,1,0:T(8,128)(2,1)S(1)} %get-tuple-element.857, s32[]{:T(128)} %get-tuple-element.856, bf16[4,4,512,512]{3,2,1,0:T(8,128)(2,1)S(1)} %copy-done, f32[128,512]{1,0:T(8,128)S(1)} %get-tuple-element.764, f32[128,512]{1,0:T(8,128)S(1)} %get-tuple-element.765, ...), kind=kOutput, calls=%fused_computation.133.clone.1 | convolution fusion | flops 73138176 | bytes 11012660 | tf_op jit(solution)/shard_map/while/body/eval_jaxpr/drw,xw->drx/dot_general | solution.py:52
  131.7 2.0 multiply_reduce_fusion.58
  142.1 8.5 %fusion.219 = bf16[6,128,512]{2,1,0:T(8,128)(2,1)S(1)} fusion(bf16[6,128,512]{2,1,0:T(8,128)(2,1)S(1)} %get-tuple-element.857, s32[]{:T(128)} %get-tuple-element.856, bf16[4,4,512,512]{3,2,1,0:T(8,128)(2,1)S(1)} %copy-done, f32[128,512]{1,0:T(8,128)S(1)} %get-tuple-element.764, f32[128,512]{1,0:T(8,128)S(1)} %get-tuple-element.765, ...), kind=kOutput, calls=%fused_computation.133.clone.1 | convolution fusion | flops 73138176 | bytes 11012660 | tf_op jit(solution)/shard_map/while/body/eval_jaxpr/drw,xw->drx/dot_general | solution.py:52
  151.5 2.0 multiply_reduce_fusion.58
  161.9 8.5 %fusion.219 = bf16[6,128,512]{2,1,0:T(8,128)(2,1)S(1)} fusion(bf16[6,128,512]{2,1,0:T(8,128)(2,1)S(1)} %get-tuple-element.857, s32[]{:T(128)} %get-tuple-element.856, bf16[4,4,512,512]{3,2,1,0:T(8,128)(2,1)S(1)} %copy-done, f32[128,512]{1,0:T(8,128)S(1)} %get-tuple-element.764, f32[128,512]{1,0:T(8,128)S(1)} %get-tuple-element.765, ...), kind=kOutput, calls=%fused_computation.133.clone.1 | convolution fusion | flops 73138176 | bytes 11012660 | tf_op jit(solution)/shard_map/while/body/eval_jaxpr/drw,xw->drx/dot_general | solution.py:52
  171.5 101.2 %all-gather.2.cloned.1.call-done = bf16[96,128,512]{2,1,0:T(8,128)(2,1)} async-done(((bf16[6,128,512]{2,1,0:T(8,128)(2,1)}), bf16[96,128,512]{2,1,0:T(8,128)(2,1)}) %all-gather.2.cloned.1.call-update) | async-done | bytes 12582928 | tf_op jit(solution)/shard_map/all_gather | solution.py:141
  272.8 335.8 %while.27 = (s32[]{:T(128)}, f32[128,512]{1,0:T(8,128)S(1)}, f32[128,512]{1,0:T(8,128)S(1)}, s32[96,2]{0,1:T(2,128)S(1)}, s32[]{:T(128)}, /*index=5*/f32[96]{0:T...) while((s32[]{:T(128)}, f32[128,512]{1,0:T(8,128)S(1)}, ...), condition=%wide.region_59.60_spmd, body=%wide.region_54.59_spmd.sunk | while | flops 88949520 | bytes 1204658 | solution.py:153
  282.8 9.6 %conditional.2 = ((f32[128,512]{1,0:T(8,128)S(1)}, f32[128,512]{1,0:T(8,128)S(1)})) conditional(s32[]{:T(128)} %convert_element_type.1283, (f32[128,512]{1,0:T(8,128)S(1)}, f32[128,512]{1,0:T(8,128)S(1)}) %tuple.161, (s32[]{:T(128)}, f32[96]{0:T(128)S(1)}, s32[96]{0:T(128)S(1)}, f32[96,2]{0,1:T(2,128)S(1)}, bf16[96,128,512]{2,1,0:T(8,128)(2,1)}, ...), branch_computations={%region_55.55_spmd, %region_56.58_spmd} | conditional | flops 88949512 | bytes 1204415 | solution.py:147
  290.5 1.9 fusion.4
  318.3 9.6 %conditional.2 = ((f32[128,512]{1,0:T(8,128)S(1)}, f32[128,512]{1,0:T(8,128)S(1)})) conditional(s32[]{:T(128)} %convert_element_type.1283, (f32[128,512]{1,0:T(8,128)S(1)}, f32[128,512]{1,0:T(8,128)S(1)}) %tuple.161, (s32[]{:T(128)}, f32[96]{0:T(128)S(1)}, s32[96]{0:T(128)S(1)}, f32[96,2]{0,1:T(2,128)S(1)}, bf16[96,128,512]{2,1,0:T(8,128)(2,1)}, ...), branch_computations={%region_55.55_spmd, %region_56.58_spmd} | conditional | flops 88949512 | bytes 1204415 | solution.py:147
  326.0 1.9 fusion.4
  337.9 9.6 %conditional.2 = ((f32[128,512]{1,0:T(8,128)S(1)}, f32[128,512]{1,0:T(8,128)S(1)})) conditional(s32[]{:T(128)} %convert_element_type.1283, (f32[128,512]{1,0:T(8,128)S(1)}, f32[128,512]{1,0:T(8,128)S(1)}) %tuple.161, (s32[]{:T(128)}, f32[96]{0:T(128)S(1)}, s32[96]{0:T(128)S(1)}, f32[96,2]{0,1:T(2,128)S(1)}, bf16[96,128,512]{2,1,0:T(8,128)(2,1)}, ...), branch_computations={%region_55.55_spmd, %region_56.58_spmd} | conditional | flops 88949512 | bytes 1204415 | solution.py:147
  345.6 1.9 fusion.4
  357.5 9.6 %conditional.2 = ((f32[128,512]{1,0:T(8,128)S(1)}, f32[128,512]{1,0:T(8,128)S(1)})) conditional(s32[]{:T(128)} %convert_element_type.1283, (f32[128,512]{1,0:T(8,128)S(1)}, f32[128,512]{1,0:T(8,128)S(1)}) %tuple.161, (s32[]{:T(128)}, f32[96]{0:T(128)S(1)}, s32[96]{0:T(128)S(1)}, f32[96,2]{0,1:T(2,128)S(1)}, bf16[96,128,512]{2,1,0:T(8,128)(2,1)}, ...), branch_computations={%region_55.55_spmd, %region_56.58_spmd} | conditional | flops 88949512 | bytes 1204415 | solution.py:147
  365.2 1.9 fusion.4
  377.1 9.6 %conditional.2 = ((f32[128,512]{1,0:T(8,128)S(1)}, f32[128,512]{1,0:T(8,128)S(1)})) conditional(s32[]{:T(128)} %convert_element_type.1283, (f32[128,512]{1,0:T(8,128)S(1)}, f32[128,512]{1,0:T(8,128)S(1)}) %tuple.161, (s32[]{:T(128)}, f32[96]{0:T(128)S(1)}, s32[96]{0:T(128)S(1)}, f32[96,2]{0,1:T(2,128)S(1)}, bf16[96,128,512]{2,1,0:T(8,128)(2,1)}, ...), branch_computations={%region_55.55_spmd, %region_56.58_spmd} | conditional | flops 88949512 | bytes 1204415 | solution.py:147
  384.8 1.9 fusion.4
  394.7 9.6 %conditional.2 = ((f32[128,512]{1,0:T(8,128)S(1)}, f32[128,512]{1,0:T(8,128)S(1)})) conditional(s32[]{:T(128)} %convert_element_type.1283, (f32[128,512]{1,0:T(8,128)S(1)}, f32[128,512]{1,0:T(8,128)S(1)}) %tuple.161, (s32[]{:T(128)}, f32[96]{0:T(128)S(1)}, s32[96]{0:T(128)S(1)}, f32[96,2]{0,1:T(2,128)S(1)}, bf16[96,128,512]{2,1,0:T(8,128)(2,1)}, ...), branch_computations={%region_55.55_spmd, %region_56.58_spmd} | conditional | flops 88949512 | bytes 1204415 | solution.py:147
  402.4 1.9 fusion.4
  416.3 9.6 %conditional.2 = ((f32[128,512]{1,0:T(8,128)S(1)}, f32[128,512]{1,0:T(8,128)S(1)})) conditional(s32[]{:T(128)} %convert_element_type.1283, (f32[128,512]{1,0:T(8,128)S(1)}, f32[128,512]{1,0:T(8,128)S(1)}) %tuple.161, (s32[]{:T(128)}, f32[96]{0:T(128)S(1)}, s32[96]{0:T(128)S(1)}, f32[96,2]{0,1:T(2,128)S(1)}, bf16[96,128,512]{2,1,0:T(8,128)(2,1)}, ...), branch_computations={%region_55.55_spmd, %region_56.58_spmd} | conditional | flops 88949512 | bytes 1204415 | solution.py:147
  437.9 9.6 %conditional.2 = ((f32[128,512]{1,0:T(8,128)S(1)}, f32[128,512]{1,0:T(8,128)S(1)})) conditional(s32[]{:T(128)} %convert_element_type.1283, (f32[128,512]{1,0:T(8,128)S(1)}, f32[128,512]{1,0:T(8,128)S(1)}) %tuple.161, (s32[]{:T(128)}, f32[96]{0:T(128)S(1)}, s32[96]{0:T(128)S(1)}, f32[96,2]{0,1:T(2,128)S(1)}, bf16[96,128,512]{2,1,0:T(8,128)(2,1)}, ...), branch_computations={%region_55.55_spmd, %region_56.58_spmd} | conditional | flops 88949512 | bytes 1204415 | solution.py:147
  445.6 1.9 fusion.4
  465.4 9.6 %conditional.2 = ((f32[128,512]{1,0:T(8,128)S(1)}, f32[128,512]{1,0:T(8,128)S(1)})) conditional(s32[]{:T(128)} %convert_element_type.1283, (f32[128,512]{1,0:T(8,128)S(1)}, f32[128,512]{1,0:T(8,128)S(1)}) %tuple.161, (s32[]{:T(128)}, f32[96]{0:T(128)S(1)}, s32[96]{0:T(128)S(1)}, f32[96,2]{0,1:T(2,128)S(1)}, bf16[96,128,512]{2,1,0:T(8,128)(2,1)}, ...), branch_computations={%region_55.55_spmd, %region_56.58_spmd} | conditional | flops 88949512 | bytes 1204415 | solution.py:147
  473.2 1.9 fusion.4
  487.0 9.6 %conditional.2 = ((f32[128,512]{1,0:T(8,128)S(1)}, f32[128,512]{1,0:T(8,128)S(1)})) conditional(s32[]{:T(128)} %convert_element_type.1283, (f32[128,512]{1,0:T(8,128)S(1)}, f32[128,512]{1,0:T(8,128)S(1)}) %tuple.161, (s32[]{:T(128)}, f32[96]{0:T(128)S(1)}, s32[96]{0:T(128)S(1)}, f32[96,2]{0,1:T(2,128)S(1)}, bf16[96,128,512]{2,1,0:T(8,128)(2,1)}, ...), branch_computations={%region_55.55_spmd, %region_56.58_spmd} | conditional | flops 88949512 | bytes 1204415 | solution.py:147
  494.7 1.9 fusion.4
  512.6 9.6 %conditional.2 = ((f32[128,512]{1,0:T(8,128)S(1)}, f32[128,512]{1,0:T(8,128)S(1)})) conditional(s32[]{:T(128)} %convert_element_type.1283, (f32[128,512]{1,0:T(8,128)S(1)}, f32[128,512]{1,0:T(8,128)S(1)}) %tuple.161, (s32[]{:T(128)}, f32[96]{0:T(128)S(1)}, s32[96]{0:T(128)S(1)}, f32[96,2]{0,1:T(2,128)S(1)}, bf16[96,128,512]{2,1,0:T(8,128)(2,1)}, ...), branch_computations={%region_55.55_spmd, %region_56.58_spmd} | conditional | flops 88949512 | bytes 1204415 | solution.py:147
  528.2 9.6 %conditional.2 = ((f32[128,512]{1,0:T(8,128)S(1)}, f32[128,512]{1,0:T(8,128)S(1)})) conditional(s32[]{:T(128)} %convert_element_type.1283, (f32[128,512]{1,0:T(8,128)S(1)}, f32[128,512]{1,0:T(8,128)S(1)}) %tuple.161, (s32[]{:T(128)}, f32[96]{0:T(128)S(1)}, s32[96]{0:T(128)S(1)}, f32[96,2]{0,1:T(2,128)S(1)}, bf16[96,128,512]{2,1,0:T(8,128)(2,1)}, ...), branch_computations={%region_55.55_spmd, %region_56.58_spmd} | conditional | flops 88949512 | bytes 1204415 | solution.py:147
  553.8 9.6 %conditional.2 = ((f32[128,512]{1,0:T(8,128)S(1)}, f32[128,512]{1,0:T(8,128)S(1)})) conditional(s32[]{:T(128)} %convert_element_type.1283, (f32[128,512]{1,0:T(8,128)S(1)}, f32[128,512]{1,0:T(8,128)S(1)}) %tuple.161, (s32[]{:T(128)}, f32[96]{0:T(128)S(1)}, s32[96]{0:T(128)S(1)}, f32[96,2]{0,1:T(2,128)S(1)}, bf16[96,128,512]{2,1,0:T(8,128)(2,1)}, ...), branch_computations={%region_55.55_spmd, %region_56.58_spmd} | conditional | flops 88949512 | bytes 1204415 | solution.py:147
  569.4 9.6 %conditional.2 = ((f32[128,512]{1,0:T(8,128)S(1)}, f32[128,512]{1,0:T(8,128)S(1)})) conditional(s32[]{:T(128)} %convert_element_type.1283, (f32[128,512]{1,0:T(8,128)S(1)}, f32[128,512]{1,0:T(8,128)S(1)}) %tuple.161, (s32[]{:T(128)}, f32[96]{0:T(128)S(1)}, s32[96]{0:T(128)S(1)}, f32[96,2]{0,1:T(2,128)S(1)}, bf16[96,128,512]{2,1,0:T(8,128)(2,1)}, ...), branch_computations={%region_55.55_spmd, %region_56.58_spmd} | conditional | flops 88949512 | bytes 1204415 | solution.py:147
  595.0 9.6 %conditional.2 = ((f32[128,512]{1,0:T(8,128)S(1)}, f32[128,512]{1,0:T(8,128)S(1)})) conditional(s32[]{:T(128)} %convert_element_type.1283, (f32[128,512]{1,0:T(8,128)S(1)}, f32[128,512]{1,0:T(8,128)S(1)}) %tuple.161, (s32[]{:T(128)}, f32[96]{0:T(128)S(1)}, s32[96]{0:T(128)S(1)}, f32[96,2]{0,1:T(2,128)S(1)}, bf16[96,128,512]{2,1,0:T(8,128)(2,1)}, ...), branch_computations={%region_55.55_spmd, %region_56.58_spmd} | conditional | flops 88949512 | bytes 1204415 | solution.py:147
  611.4 8.4 %reduce-scatter.3.cloned.1.call-done = f32[64,512]{1,0:T(8,128)} async-done(((f32[128,512]{1,0:T(8,128)}), f32[64,512]{1,0:T(8,128)}) %reduce-scatter.3.cloned.1.call-update) | async-done | bytes 131088 | tf_op jit(solution)/shard_map/reduce_scatter | solution.py:155
  619.7 14.0 %reduce-scatter.5.cloned.1.call-done = f32[64,512]{1,0:T(8,128)} async-done(((f32[128,512]{1,0:T(8,128)}), f32[64,512]{1,0:T(8,128)}) %reduce-scatter.5.cloned.1.call-update) | async-done | bytes 131088 | tf_op jit(solution)/shard_map/reduce_scatter | solution.py:156
  634.8 2.2 collective-permute-start
  638.3 3.1 collective-permute-done.1
  641.4 5.3 collective-permute-start.2
  646.7 1.9 collective-permute-start.3
  649.3 3.6 collective-permute-done.3
  653.0 5.7 fusion.128
  658.7 6.5 fusion.136
  (568 shorter events, 229.9 us)
Async XLA Ops:
  7.2 43.7 %copy-start.4 = (bf16[1,6,128,512]{3,2,1,0:T(8,128)(2,1)S(1)}, bf16[1,6,128,512]{3,2,1,0:T(8,128)(2,1)}, u32[]{:S(2)}) copy-start(bf16[1,6,128,512]{3,2,1,0:T(8,128)(2,1)} %param.13) | copy-start | bytes 2359300
  7.2 44.1 %copy-start.8 = (f32[1,6,3,40]{3,0,2,1:T(1,128)S(1)}, f32[1,6,3,40]{3,0,2,1:T(1,128)}, u32[]{:S(2)}) copy-start(f32[1,6,3,40]{3,0,2,1:T(1,128)} %param.14) | copy-start | bytes 8644
  7.2 265.5 %all-gather.2.cloned.1.call-start = ((), (), s32[]{:S(2)}) async-start(), calls=%async_computation.2 | async-start | bytes 13369344 | tf_op jit(solution)/shard_map/all_gather | solution.py:141
  51.3 221.5 %copy-start.6 = (s32[1,96,2]{1,2,0:T(2,128)S(1)}, s32[1,96,2]{1,2,0:T(2,128)}, u32[]{:S(2)}) copy-start(s32[1,96,2]{1,2,0:T(2,128)} %param.15) | copy-start | bytes 2308
  51.3 221.5 %copy-start.7 = (f32[1,96,2]{1,2,0:T(2,128)S(1)}, f32[1,96,2]{1,2,0:T(2,128)}, u32[]{:S(2)}) copy-start(f32[1,96,2]{1,2,0:T(2,128)} %param.18) | copy-start | bytes 2308
  51.3 221.5 %copy-start.9 = (f32[1,96]{1,0:T(1,128)S(1)}, f32[1,96]{1,0:T(1,128)}, u32[]{:S(2)}) copy-start(f32[1,96]{1,0:T(1,128)} %param.19) | copy-start | bytes 1156
  51.3 221.5 %copy-start.10 = (s32[1,96]{1,0:T(1,128)S(1)}, s32[1,96]{1,0:T(1,128)}, u32[]{:S(2)}) copy-start(s32[1,96]{1,0:T(1,128)} %param.16) | copy-start | bytes 1156
  51.3 221.5 %copy-start.11 = (s32[1,96]{1,0:T(1,128)S(1)}, s32[1,96]{1,0:T(1,128)}, u32[]{:S(2)}) copy-start(s32[1,96]{1,0:T(1,128)} %param.17) | copy-start | bytes 1156
  51.5 4.7 copy-start
  71.3 4.7 copy-start
  91.2 4.7 copy-start
  111.0 4.7 copy-start
  130.8 4.7 copy-start
  150.7 4.7 copy-start
  170.5 0.9 copy-start.5
  171.4 448.3 %reduce-scatter.3.cloned.1.call-start = ((), (), s32[]{:S(2)}) async-start(), calls=%async_computation.3 | async-start | bytes 393216 | tf_op jit(solution)/shard_map/reduce_scatter | solution.py:155
  608.6 0.7 copy-start.3
  608.6 0.8 copy-start.1
  609.3 24.4 %reduce-scatter.5.cloned.1.call-start = ((), (), s32[]{:S(2)}) async-start(), calls=%async_computation.4 | async-start | bytes 393216 | tf_op jit(solution)/shard_map/reduce_scatter | solution.py:156
  634.7 30.5 %copy-start.2 = (f32[64,512]{1,0:T(8,128)}, f32[64,512]{1,0:T(8,128)S(1)}, u32[]{:S(2)}) copy-start(f32[64,512]{1,0:T(8,128)S(1)} %maximum_divide_fusion) | copy-start | bytes 393220
  634.8 3.5 collective-permute-start
  636.9 4.4 collective-permute-start.1
  641.4 7.9 %collective-permute-start.2 = (f32[72,4]{1,0:T(8,128)S(1)}, f32[72,4]{1,0:T(8,128)S(1)}, u32[]{:S(2)}, u32[]{:S(2)}) collective-permute-start(f32[72,4]{1,0:T(8,128)S(1)} %get-tuple-element.558), channel_id=1, source_target_pairs={{0,1},{1,2},{2,3},{3,4},{4,5},{5,6},{6,7},{7,8},{8,9},{9,10},{10,1... | collective-permute-start | bytes 3464 | tf_op jit(solution)/shard_map/ppermute | solution.py:18
  646.7 6.2 collective-permute-start.3
Sparse Core Ops, SparseCore 0:
  171.6 101.1 all-gather.1
  609.4 10.2 reduce-scatter.2
  622.0 11.7 reduce-scatter.4
where the time goes:
time: 676 us; the launch traced here: 672 us
  loops' own time  185 us (27%)
  matrix products  141 us (21%)
  waiting for transfers between devices  131 us (19%)
  local copies, waits for them, and re-layouts  107 us (16%)
  other arithmetic  71.6 us (11%)
  between operations  25.4 us (4%)
  starting transfers between devices  10.8 us (2%)
    another operation x1, loops' own time, local(): flux_sum, cover_sum = lax.fori_loop(0, arrived.shape[0], visit_one, empty)  128 us
    dot_general x96, matrix products, match_exposure(): jnp.einsum('drw,xw->drx', smoothed[group, :count], col_band[group, x_degr...  108 us
    all_gather x1, waiting for transfers between devices, local(): arrived = lax.all_gather(matched, 'patch', axis=0, tiled=True)  101 us
    dynamic_slice x96, local copies, waits for them, and re-layouts, visit_one(): hit_second = table[offset, 1] == own_patch  62.7 us
    another operation x96, loops' own time, visit_one(): lax.cond(hit_first | hit_second, lambda: add_exposure(inner, exposure, of...  56 us
    dot_general x15, matrix products, warp_exposure(): warped = jnp.dot(middle, col_map, preferred_element_type=jnp.float32)  28.8 us
    unnamed x30, other arithmetic  21.1 us
    reduce_scatter x1, waiting for transfers between devices, local(): lax.psum_scatter(cover_sum, 'visit', scatter_dimension=0, tiled=True)  14 us
  transfers between devices with their start and end apart: 7, of which 5 were waited for; matrix products, arithmetic and copies ran while one was open for 0% of the time, Pallas kernels for 0%

commit v1 on v0

--- a/solution.py
+++ b/solution.py
@@ -138,7 +138,17 @@
         )
         return (totals[0] + flux_part, totals[1] + cover_part)
 
-    arrived = lax.all_gather(matched, "patch", axis=0, tiled=True)
+    val2 = lax.axis_index("patch")
+    w2 = lax.axis_size("patch")
+    o_now, formed, block_now = (w2, val2, matched.shape[0])
+    part_next, y_new = (matched, 1)
+    while y_new < o_now:
+        everything = lax.ppermute(
+            part_next, axis_name="patch", perm=[(t, (t - y_new) % o_now) for t in range(o_now)]
+        )
+        part_next = jnp.concatenate([part_next, everything], axis=0)
+        y_new = 2 * y_new
+    arrived = jnp.roll(part_next, formed * block_now, axis=0)
 
     def visit_one(offset, inner):
         hit_first = table[offset, 0] == own_patch

time: 676 us -> 992 us (1.47)
  waiting for transfers between devices: 131 us -> 405 us
  local copies, waits for them, and re-layouts: 107 us -> 140 us
  loops' own time: 185 us -> 175 us
    ppermute x0 -> x4, waiting for transfers between devices: none -> 376 us  [local(): lax.ppermute(part_next, axis_name='patch', perm=[(t, (t - y_new) % o_now)...]
    all_gather x1 -> x0, waiting for transfers between devices: 101 us -> none  [local(): arrived = lax.all_gather(matched, 'patch', axis=0, tiled=True)]
    unnamed x24 -> x43, local copies, waits for them, and re-layouts: 2.04 us -> 21.4 us
    dynamic_slice x0 -> x1, local copies, waits for them, and re-layouts: none -> 10.7 us  [local(): arrived = jnp.roll(part_next, formed * block_now, axis=0)]
  transfers between devices with their start and end apart: 7 -> 10, of which waited for: 5 -> 8; matrix products, arithmetic and copies ran while one was open for 0% -> 1% of each run, Pallas kernels for 0% -> 0%
where the time goes in v1:
time: 992 us; the launch traced here: 981 us
  waiting for transfers between devices  405 us (41%)
  loops' own time  175 us (18%)
  matrix products  141 us (14%)
  local copies, waits for them, and re-layouts  140 us (14%)
  other arithmetic  77 us (8%)
  between operations  25.7 us (3%)
  starting transfers between devices  17.6 us (2%)
    ppermute x4, waiting for transfers between devices, local(): lax.ppermute(part_next, axis_name='patch', perm=[(t, (t - y_new) % o_now)...  376 us
    another operation x1, loops' own time, local(): flux_sum, cover_sum = lax.fori_loop(0, arrived.shape[0], visit_one, empty)  118 us
    dot_general x96, matrix products, match_exposure(): jnp.einsum('drw,xw->drx', smoothed[group, :count], col_band[group, x_degr...  108 us
    dynamic_slice x96, local copies, waits for them, and re-layouts, visit_one(): hit_second = table[offset, 1] == own_patch  59.1 us
    another operation x96, loops' own time, visit_one(): lax.cond(hit_first | hit_second, lambda: add_exposure(inner, exposure, of...  56.2 us
    dot_general x15, matrix products, warp_exposure(): warped = jnp.dot(middle, col_map, preferred_element_type=jnp.float32)  29 us
    unnamed x43, local copies, waits for them, and re-layouts  21.4 us
    unnamed x30, other arithmetic  21.1 us
  transfers between devices with their start and end apart: 10, of which 8 were waited for; matrix products, arithmetic and copies ran while one was open for 1% of the time, Pallas kernels for 0%

profile of v1, /device:TPU:5, one launch (start us, length us, event | category | flops | bytes accessed | tf_op | source)
XLA Modules:
  0.0 981.5 jit_solution(7296078706080223551)
XLA Ops:
  51.2 119.1 %while.28 = (s32[]{:T(128)}, bf16[6,128,512]{2,1,0:T(8,128)(2,1)S(1)}, f32[6,3,40]{2,1,0:T(4,128)S(1)}, bf16[6,128,512]{1,2,0:T(8,128)(2,1)S(1)}, bf16[4,4,128,1...) while((s32[]{:T(128)}, ...), condition=%wide.region_53.54_spmd.clone.clone, body=%wide.region_16.53_spmd.clone.clone.sunk | while | flops 2971667456 | bytes 70542368 | solution.py:123
  62.7 8.5 fusion.219
  72.1 2.0 multiply_reduce_fusion.58
  82.5 8.5 fusion.219
  91.9 2.0 multiply_reduce_fusion.58
  102.4 8.5 fusion.219
  111.7 2.0 multiply_reduce_fusion.58
  122.2 8.5 fusion.219
  131.6 2.0 multiply_reduce_fusion.58
  142.0 8.5 fusion.219
  151.4 2.0 multiply_reduce_fusion.58
  161.8 8.5 fusion.219
  171.1 11.6 %collective-permute-done = bf16[6,128,512]{2,1,0:T(8,128)(2,1)S(1)} collective-permute-done((bf16[6,128,512]{2,1,0:T(8,128)(2,1)S(1)}, bf16[6,128,512]{2,1,0:T(8,128)(2,1)S(1)}, u32[]{:S(2)}, u32[]{:S(2)}) %collective-permute-start) | collective-permute-done | bytes 786464 | tf_op jit(solution)/shard_map/ppermute | solution.py:146
  183.0 35.3 %collective-permute-done.1 = bf16[12,128,512]{2,1,0:T(8,128)(2,1)S(1)} collective-permute-done((bf16[12,128,512]{2,1,0:T(8,128)(2,1)S(1)}, bf16[12,128,512]{2,1,0:T(8,128)(2,1)S(1)}, u32[]{:S(2)}, u32[]{:S(2)}) %collective-permute-start.1) | collective-permute-done | bytes 1572896 | tf_op jit(solution)/shard_map/ppermute | solution.py:146
  218.6 5.2 collective-permute-start.2
  223.8 65.6 %collective-permute-done.2 = bf16[24,128,512]{2,1,0:T(8,128)(2,1)S(1)} collective-permute-done((bf16[24,128,512]{2,1,0:T(8,128)(2,1)S(1)}, bf16[24,128,512]{2,1,0:T(8,128)(2,1)S(1)}, u32[]{:S(2)}, u32[]{:S(2)}) %collective-permute-start.2) | collective-permute-done | bytes 3145760 | tf_op jit(solution)/shard_map/ppermute | solution.py:146
  289.4 4.5 pad_maximum_fusion
  294.8 2.1 constant_dynamic-update-slice_fusion.25
  296.9 2.1 constant_dynamic-update-slice_fusion.24
  299.0 2.7 constant_dynamic-update-slice_fusion.23
  303.7 263.2 %collective-permute-done.3 = bf16[48,128,512]{2,1,0:T(8,128)(2,1)} collective-permute-done((bf16[48,128,512]{2,1,0:T(8,128)(2,1)}, bf16[48,128,512]{2,1,0:T(8,128)(2,1)}, u32[]{:S(2)}, u32[]{:S(2)}) %collective-permute-start.3) | collective-permute-done | bytes 6291488 | tf_op jit(solution)/shard_map/ppermute | solution.py:146
  566.9 6.1 constant_dynamic-update-slice_fusion.21
  578.3 6.1 constant_dynamic-update-slice_fusion.16
  584.4 10.7 %constant_dynamic-slice_fusion.4 = bf16[96,128,512]{2,1,0:T(8,128)(2,1)} fusion(bf16[192,128,512]{2,1,0:T(8,128)(2,1)} %constant_dynamic-update-slice_fusion.16, s32[]{:T(128)S(6)} %select_n.407), kind=kLoop, calls=%fused_computation.423 | loop fusion | bytes 25165828 | tf_op jit(solution)/shard_map/jit(_roll_dynamic)/dynamic_slice | solution.py:151
  595.2 323.2 %while.27 = (s32[]{:T(128)}, f32[128,512]{1,0:T(8,128)S(1)}, f32[128,512]{1,0:T(8,128)S(1)}, s32[96,2]{0,1:T(2,128)S(1)}, s32[]{:T(128)}, /*index=5*/f32[96]{0:T...) while((s32[]{:T(128)}, f32[128,512]{1,0:T(8,128)S(1)}, ...), condition=%wide.region_59.60_spmd, body=%wide.region_54.59_spmd.sunk | while | flops 88949520 | bytes 1204658 | solution.py:163
  604.4 9.7 conditional.2
  638.2 9.7 conditional.2
  657.1 9.7 conditional.2
  676.1 9.7 conditional.2
  695.0 9.7 conditional.2
  712.1 9.7 conditional.2
  732.9 9.7 conditional.2
  753.7 9.7 conditional.2
  780.1 9.7 conditional.2
  800.9 9.7 conditional.2
  825.4 9.7 conditional.2
  840.7 9.7 conditional.2
  865.2 9.7 conditional.2
  880.4 9.7 conditional.2
  904.9 9.7 conditional.2
  921.1 8.0 reduce-scatter.3.cloned.1.call-done
  929.1 14.0 %reduce-scatter.5.cloned.1.call-done = f32[64,512]{1,0:T(8,128)} async-done(((f32[128,512]{1,0:T(8,128)}), f32[64,512]{1,0:T(8,128)}) %reduce-scatter.5.cloned.1.call-update) | async-done | bytes 131088 | tf_op jit(solution)/shard_map/reduce_scatter | solution.py:166
  944.2 2.2 collective-permute-start.4
  947.7 3.1 collective-permute-done.5
  950.8 5.2 collective-permute-start.6
  958.7 3.6 collective-permute-done.7
  962.4 5.7 fusion.128
  968.1 6.5 fusion.136
  (597 shorter events, 256.5 us)
Async XLA Ops:
  7.2 43.7 %copy-start.10 = (bf16[1,6,128,512]{3,2,1,0:T(8,128)(2,1)S(1)}, bf16[1,6,128,512]{3,2,1,0:T(8,128)(2,1)}, u32[]{:S(2)}) copy-start(bf16[1,6,128,512]{3,2,1,0:T(8,128)(2,1)} %param.13) | copy-start | bytes 2359300
  7.2 44.1 %copy-start.13 = (f32[1,6,3,40]{3,0,2,1:T(1,128)S(1)}, f32[1,6,3,40]{3,0,2,1:T(1,128)}, u32[]{:S(2)}) copy-start(f32[1,6,3,40]{3,0,2,1:T(1,128)} %param.14) | copy-start | bytes 8644
  7.2 921.9 %reduce-scatter.3.cloned.1.call-start = ((), (), s32[]{:S(2)}) async-start(), calls=%async_computation.2 | async-start | bytes 393216 | tf_op jit(solution)/shard_map/reduce_scatter | solution.py:165
  51.4 4.7 copy-start.6
  71.3 4.7 copy-start.6
  91.1 4.7 copy-start.6
  110.9 4.7 copy-start.6
  130.7 4.7 copy-start.6
  150.6 4.7 copy-start.6
  170.4 47.9 %copy-start.2 = (bf16[6,128,512]{2,1,0:T(8,128)(2,1)}, bf16[6,128,512]{2,1,0:T(8,128)(2,1)S(1)}, u32[]{:S(2)}) copy-start(bf16[6,128,512]{2,1,0:T(8,128)(2,1)S(1)} %get-tuple-element.365) | copy-start | bytes 2359300
  170.4 12.4 %collective-permute-start = (bf16[6,128,512]{2,1,0:T(8,128)(2,1)S(1)}, bf16[6,128,512]{2,1,0:T(8,128)(2,1)S(1)}, u32[]{:S(2)}, u32[]{:S(2)}) collective-permute-start(bf16[6,128,512]{2,1,0:T(8,128)(2,1)S(1)} %get-tuple-element.365), channel_id=1, source_target_pairs={{0,15},{1,0},{2,1},{3,2},{4,3},{5,4},{6,5},{7,6},{8,7},{9,8},{10,9... | collective-permute-start | bytes 2359304 | tf_op jit(solution)/shard_map/ppermute | solution.py:146
  182.8 111.2 %copy-start.4 = (bf16[6,128,512]{2,1,0:T(8,128)(2,1)}, bf16[6,128,512]{2,1,0:T(8,128)(2,1)S(1)}, u32[]{:S(2)}) copy-start(bf16[6,128,512]{2,1,0:T(8,128)(2,1)S(1)} %collective-permute-done) | copy-start | bytes 2359300
  182.9 35.4 %collective-permute-start.1 = (bf16[12,128,512]{2,1,0:T(8,128)(2,1)S(1)}, bf16[12,128,512]{2,1,0:T(8,128)(2,1)S(1)}, u32[]{:S(2)}, u32[]{:S(2)}) collective-permute-start(bf16[12,128,512]{2,1,0:T(8,128)(2,1)S(1)} %pad_maximum_fusion.2), channel_id=1, source_target_pairs={{0,14},{1,15},{2,0},{3,1},{4,2},{5,3},{6,4},{7,5},{8,6},{9,7},{10,... | collective-permute-start | bytes 4718600 | tf_op jit(solution)/shard_map/ppermute | solution.py:146
  218.3 75.6 %copy-start = (bf16[12,128,512]{2,1,0:T(8,128)(2,1)}, bf16[12,128,512]{2,1,0:T(8,128)(2,1)S(1)}, u32[]{:S(2)}) copy-start(bf16[12,128,512]{2,1,0:T(8,128)(2,1)S(1)} %collective-permute-done.1) | copy-start | bytes 4718596
  218.6 70.8 %collective-permute-start.2 = (bf16[24,128,512]{2,1,0:T(8,128)(2,1)S(1)}, bf16[24,128,512]{2,1,0:T(8,128)(2,1)S(1)}, u32[]{:S(2)}, u32[]{:S(2)}) collective-permute-start(bf16[24,128,512]{2,1,0:T(8,128)(2,1)S(1)} %pad_maximum_fusion.1), channel_id=1, source_target_pairs={{0,12},{1,13},{2,14},{3,15},{4,0},{5,1},{6,2},{7,3},{8,4},{9,5},{1... | collective-permute-start | bytes 9437192 | tf_op jit(solution)/shard_map/ppermute | solution.py:146
  293.9 273.0 %collective-permute-start.3 = (bf16[48,128,512]{2,1,0:T(8,128)(2,1)}, bf16[48,128,512]{2,1,0:T(8,128)(2,1)}, u32[]{:S(2)}, u32[]{:S(2)}) collective-permute-start(bf16[48,128,512]{2,1,0:T(8,128)(2,1)} %pad_maximum_fusion), channel_id=1, source_target_pairs={{0,8},{1,9},{2,10},{3,11},{4,12},{5,13},{6,14},{7,15},{8,0},{9,1},... | collective-permute-start | bytes 18874376 | tf_op jit(solution)/shard_map/ppermute | solution.py:146
  301.7 271.3 %copy-start.3 = (bf16[6,128,512]{2,1,0:T(8,128)(2,1)S(1)}, bf16[6,128,512]{2,1,0:T(8,128)(2,1)}, u32[]{:S(2)}) copy-start(bf16[6,128,512]{2,1,0:T(8,128)(2,1)} %copy-done.2) | copy-start | bytes 2359300
  303.7 270.4 %copy-start.5 = (bf16[6,128,512]{2,1,0:T(8,128)(2,1)S(1)}, bf16[6,128,512]{2,1,0:T(8,128)(2,1)}, u32[]{:S(2)}) copy-start(bf16[6,128,512]{2,1,0:T(8,128)(2,1)} %copy-done.4) | copy-start | bytes 2359300
  303.7 271.3 %copy-start.1 = (bf16[12,128,512]{2,1,0:T(8,128)(2,1)S(1)}, bf16[12,128,512]{2,1,0:T(8,128)(2,1)}, u32[]{:S(2)}) copy-start(bf16[12,128,512]{2,1,0:T(8,128)(2,1)} %copy-done) | copy-start | bytes 4718596
  584.4 10.7 %copy-start.11 = (s32[1,96,2]{1,2,0:T(2,128)S(1)}, s32[1,96,2]{1,2,0:T(2,128)}, u32[]{:S(2)}) copy-start(s32[1,96,2]{1,2,0:T(2,128)} %param.15) | copy-start | bytes 2308
  584.4 10.7 %copy-start.12 = (f32[1,96,2]{1,2,0:T(2,128)S(1)}, f32[1,96,2]{1,2,0:T(2,128)}, u32[]{:S(2)}) copy-start(f32[1,96,2]{1,2,0:T(2,128)} %param.18) | copy-start | bytes 2308
  584.4 10.7 %copy-start.14 = (f32[1,96]{1,0:T(1,128)S(1)}, f32[1,96]{1,0:T(1,128)}, u32[]{:S(2)}) copy-start(f32[1,96]{1,0:T(1,128)} %param.19) | copy-start | bytes 1156
  584.4 10.8 %copy-start.15 = (s32[1,96]{1,0:T(1,128)S(1)}, s32[1,96]{1,0:T(1,128)}, u32[]{:S(2)}) copy-start(s32[1,96]{1,0:T(1,128)} %param.16) | copy-start | bytes 1156
  584.4 10.8 %copy-start.16 = (s32[1,96]{1,0:T(1,128)S(1)}, s32[1,96]{1,0:T(1,128)}, u32[]{:S(2)}) copy-start(s32[1,96]{1,0:T(1,128)} %param.17) | copy-start | bytes 1156
  918.3 0.7 copy-start.9
  918.3 0.8 copy-start.7
  919.1 24.1 %reduce-scatter.5.cloned.1.call-start = ((), (), s32[]{:S(2)}) async-start(), calls=%async_computation.3 | async-start | bytes 393216 | tf_op jit(solution)/shard_map/reduce_scatter | solution.py:166
  944.1 30.5 %copy-start.8 = (f32[64,512]{1,0:T(8,128)}, f32[64,512]{1,0:T(8,128)S(1)}, u32[]{:S(2)}) copy-start(f32[64,512]{1,0:T(8,128)S(1)} %maximum_divide_fusion) | copy-start | bytes 393220
  944.2 3.5 collective-permute-start.4
  946.4 4.4 collective-permute-start.5
  950.8 7.9 collective-permute-start.6
  956.1 6.2 collective-permute-start.7
Sparse Core Ops, SparseCore 0:
  919.2 9.8 reduce-scatter.2
  931.3 11.7 reduce-scatter.4
